TPU v7x, 128 devices: a whole 4x4x4 slice. The times are simulated.
128 devices in a mesh: dp: 32 (over z, y, core), section: 4 (over x).
Axes of the slice: x: 4, y: 4, z: 4, core: 2. Of those that a mesh axis runs over, the one named last changes fastest.
Arguments:
- real_in: bfloat16 [256, 144, 512], P('dp'), may hold values from -48 to 48
- fake_in: bfloat16 [256, 144, 512], P('dp'), may hold values from -48 to 48
- kernel_first: bfloat16 [5, 512, 1024], P(None, None, 'section'), may hold values from -0.15625 to 0.15625
- kernel_second: bfloat16 [5, 1024, 1024], P(None, None, 'section'), may hold values from -0.125 to 0.125
Outputs:
- layer_loss: float32 [2], replicated
- grad_first: float32 [512, 5, 1024], P('dp', None, 'section')
- grad_second: float32 [1024, 5, 1024], P('dp', None, 'section')
All inputs are finite; a program needn't handle non-finite values.
Results may differ from a plain program's by a relative error of at most 0.012.
The roundings to bfloat16 on the way count: a program that leaves them out, or rounds other values in their place, can miss the bound.
Values may be sent and summed in bfloat16 or wider, within the bound.
No kernel may reach another device: no remote copies, remote signals or barrier semaphores. Data moves between devices by JAX's collectives and lax.ppermute only.
A program may use at most 128 MiB of HBM per device.

v0:
```python
import jax
import jax.numpy as jnp
from jax import lax
from jax.sharding import Mesh
from jax.sharding import PartitionSpec as P

K = 5
DP = ("dp_0", "dp_1", "dp_2")
DP_SECTION = ("dp_0", "dp_1", "dp_2", "section")
smooth_width = 0.1
leak_slope = 0.1


def copy_for_each(x, axis):
    count = lax.axis_size(axis)
    return lax.all_to_all(jnp.broadcast_to(x[None], (count, *x.shape)), axis, 0, 0, tiled=True)


def in_order(blocks, dim):
    shape = list(blocks.shape[1:])
    shape[dim] *= blocks.shape[0]
    return jnp.moveaxis(blocks, 0, dim).reshape(shape)


def gathered_copies(x, axis, dim):
    blocks = copy_for_each(x, axis)
    return in_order(blocks, dim)


def one_axis_at_a_time(x, axes):
    for axis in axes:
        x = lax.psum(x, axis)
    return x


def in_blocks(x, dim, count):
    shape = x.shape
    blocks = x.reshape(*shape[:dim], count, shape[dim] // count, *shape[dim + 1 :])
    return jnp.moveaxis(blocks, dim, 0)


def sum_packed(arrays, axis, dims):
    count = lax.axis_size(axis)
    blocks = [in_blocks(a, dim, count) for a, dim in zip(arrays, dims)]
    lines = jnp.concatenate([b.reshape(count, -1) for b in blocks], axis=1)
    span = max(16, -(-lines.shape[1] // 1024) * 8)
    lines = jnp.pad(lines, ((0, 0), (0, span * 128 - lines.shape[1]))).reshape(-1, 128)
    vector, at, finished = (lax.psum_scatter(lines, axis, tiled=True).reshape(-1), 0, [])
    for b in blocks:
        part = b[0]
        finished.append(vector[at : at + part.size].reshape(part.shape))
        at += part.size
    return tuple(finished)


def conv_strided(values, kernel, frames):
    padded = jnp.pad(values, ((0, 0), (2, 2), (0, 0)))
    summed = jnp.zeros((values.shape[0] * frames, kernel.shape[2]), jnp.float32)
    for tap in range(kernel.shape[0]):
        window = padded[:, tap : tap + 3 * frames - 2 : 3].reshape(-1, values.shape[2])
        summed = summed + jnp.dot(window, kernel[tap], preferred_element_type=jnp.float32)
    return summed.reshape(values.shape[0], frames, -1)


def conv_forward(values, kernel):
    frames = values.shape[1]
    padded = jnp.pad(values, ((0, 0), (2, 2), (0, 0)))
    summed = jnp.zeros((values.shape[0] * frames, kernel.shape[2]), jnp.float32)
    for tap in range(kernel.shape[0]):
        window = padded[:, tap : tap + frames].reshape(-1, values.shape[2])
        summed = summed + jnp.dot(window, kernel[tap], preferred_element_type=jnp.float32)
    return summed.reshape(values.shape[0], frames, -1)


def conv_backward(delta, kernel):
    frames = delta.shape[1]
    padded = jnp.pad(delta, ((0, 0), (2, 2), (0, 0)))
    summed = jnp.zeros((delta.shape[0] * frames, kernel.shape[1]), jnp.float32)
    for tap in range(kernel.shape[0]):
        window = padded[:, 4 - tap : 4 - tap + frames].reshape(-1, delta.shape[2])
        summed = summed + lax.dot_general(
            window, kernel[tap], (((1,), (1,)), ((), ())), preferred_element_type=jnp.float32
        )
    return summed.reshape(delta.shape[0], frames, -1)


def weight_term(values, delta, amount, stride):
    frames = delta.shape[1]
    padded = jnp.pad(values, ((0, 0), (2, 2), (0, 0)))
    flat_delta = delta.reshape(-1, delta.shape[2])
    pieces = []
    for tap in range(K):
        window = padded[:, tap : tap + stride * (frames - 1) + 1 : stride].reshape(-1, amount)
        pieces.append(
            lax.dot_general(
                window, flat_delta, (((0,), (0,)), ((), ())), preferred_element_type=jnp.float32
            )
        )
    return jnp.stack(pieces, axis=1)


def activate(pre):
    return jnp.where(pre > 0, pre, leak_slope * pre).astype(jnp.bfloat16)


def local_grad(feature, normaliser):
    half = feature.shape[0] // 2
    difference = feature[:half].astype(jnp.float32) - feature[half:].astype(jnp.float32)
    slope = (
        difference / jnp.sqrt(difference * difference + smooth_width * smooth_width) / normaliser
    )
    return jnp.concatenate([slope, -slope], axis=0)


def smooth_total(feature):
    half = feature.shape[0] // 2
    difference = feature[:half].astype(jnp.float32) - feature[half:].astype(jnp.float32)
    return jnp.sum(jnp.sqrt(difference * difference + smooth_width * smooth_width) - smooth_width)


def shards(real_in, fake_in, kernel_first, kernel_second):
    replicas = lax.axis_size(DP)
    frames = real_in.shape[1] // 3
    in_width = real_in.shape[2]
    width = kernel_second.shape[1]
    normaliser = float(real_in.shape[0] * frames)
    count_all = float(real_in.shape[0] * replicas * frames * width)
    values = jnp.concatenate([real_in, fake_in], axis=0)
    first = activate(conv_strided(values, kernel_first, frames))
    partial_first = smooth_total(first)
    whole_first = gathered_copies(first, "section", 2)
    second = activate(conv_forward(whole_first, kernel_second))
    partial_second = smooth_total(second)
    total_first, total_second = (
        one_axis_at_a_time(partial_first, DP_SECTION),
        one_axis_at_a_time(partial_second, DP_SECTION),
    )
    layer_loss = jnp.stack([total_first, total_second]) / count_all
    delta_second = (local_grad(second, normaliser) * jnp.where(second > 0, 1.0, leak_slope)).astype(
        jnp.bfloat16
    )
    upstream_terms = conv_backward(delta_second, kernel_second)
    upstream = lax.psum_scatter(
        upstream_terms.astype(jnp.bfloat16), "section", scatter_dimension=2, tiled=True
    )
    delta_first = (
        (local_grad(first, normaliser) + upstream.astype(jnp.float32))
        * jnp.where(first > 0, 1.0, leak_slope)
    ).astype(jnp.bfloat16)
    term_first = weight_term(values, delta_first, in_width, 3)
    term_second = weight_term(whole_first, delta_second, width, 1)
    grad_first, grad_second = tuple(
        (
            part.astype(jnp.float32)
            for part in sum_packed(
                (term_first.astype(jnp.bfloat16), term_second.astype(jnp.bfloat16)), DP, (0, 0)
            )
        )
    )
    return (layer_loss, grad_first, grad_second)


def solution(mesh):
    finer = Mesh(
        mesh.devices.reshape(4, 4, 2, mesh.shape["section"]), ("dp_0", "dp_1", "dp_2", "section")
    )
    return jax.shard_map(
        shards,
        mesh=finer,
        in_specs=(
            P(DP, None, None),
            P(DP, None, None),
            P(None, None, "section"),
            P(None, None, "section"),
        ),
        out_specs=(P(), P(DP, None, "section"), P(DP, None, "section")),
        check_vma=False,
    )
```

profile of v0, /device:TPU:0, one launch (start us, length us, event | category | flops | bytes accessed | tf_op | source)
XLA Modules:
  0.0 208.0 jit_solution(5430325532296938739)
XLA Ops:
  7.2 2.6 %fusion.3 = bf16[16,148,512]{2,1,0:T(8,128)(2,1)S(1)} fusion(bf16[8,144,512]{2,1,0:T(8,128)(2,1)} %param.5, bf16[8,144,512]{2,1,0:T(8,128)(2,1)} %param.4), kind=kLoop, calls=%fused_computation.7 | loop fusion | flops 10911744 | bytes 4784128 | tf_op jit(solution)/shard_map/concatenate | solution.py:128
  9.9 3.4 %slice.116 = bf16[16,48,512]{2,1,0:T(8,128)(2,1)} slice(bf16[16,148,512]{2,1,0:T(8,128)(2,1)S(1)} %fusion.3), slice={[0:16:1], [3:145:3], [0:512:1]} | slice | bytes 1572864 | tf_op jit(solution)/shard_map/slice | solution.py:60
  13.2 3.2 %slice.114 = bf16[16,48,512]{2,1,0:T(8,128)(2,1)} slice(bf16[16,148,512]{2,1,0:T(8,128)(2,1)S(1)} %fusion.3), slice={[0:16:1], [2:144:3], [0:512:1]} | slice | bytes 1572864 | tf_op jit(solution)/shard_map/slice | solution.py:60
  16.5 3.3 %slice.112 = bf16[16,48,512]{2,1,0:T(8,128)(2,1)} slice(bf16[16,148,512]{2,1,0:T(8,128)(2,1)S(1)} %fusion.3), slice={[0:16:1], [1:143:3], [0:512:1]} | slice | bytes 1572864 | tf_op jit(solution)/shard_map/slice | solution.py:60
  19.7 1.2 slice.110
  20.9 3.5 %slice.118 = bf16[16,48,512]{2,1,0:T(8,128)(2,1)} slice(bf16[16,148,512]{2,1,0:T(8,128)(2,1)S(1)} %fusion.3), slice={[0:16:1], [4:146:3], [0:512:1]} | slice | bytes 1572864 | tf_op jit(solution)/shard_map/slice | solution.py:60
  24.4 1.5 fusion.68
  25.9 1.3 convolution_add_fusion.7
  30.1 24.9 %all_to_all.5 = bf16[4,16,48,256]{3,2,1,0:T(8,128)(2,1)S(1)} all-to-all(bf16[4,16,48,256]{3,2,1,0:T(8,128)(2,1)S(1)} %broadcast_in_dim.16), channel_id=1, replica_groups=mesh['dp_0'=4,'dp_1'=4,'dp_2'=2,'section'=4] {'section'}, dimensions={0} | all-to-all | bytes 3145728 | tf_op jit(solution)/shard_map/all_to_all | solution.py:16
  55.0 1.2 copy.16
  56.8 1.5 pad_slice_fusion
  58.4 1.1 copy-done
  62.5 0.8 fusion.76
  66.8 2.0 add_convert_fusion
  69.1 2.9 %fusion.75 = (f32[8,48,256]{2,1,0:T(8,128)}, f32[8,48,256]{2,1,0:T(8,128)}, f32[]{:T(128)}) fusion(bf16[16,48,256]{2,1,0:T(8,128)(2,1)} %copy-done.6), kind=kLoop, calls=%fused_computation.123 | loop fusion | flops 983039 | bytes 1179652 | tf_op jit(solution)/shard_map/neg | solution.py:112
  72.7 0.8 copy-done.5
  76.8 3.7 %copy.19 = bf16[1024,5,256]{2,1,0:T(8,128)(2,1)} copy(bf16[1024,5,256]{2,0,1:T(8,128)(2,1)S(1)} %fusion.11) | data formatting | bytes 5242880 | tf_op jit(solution)/shard_map/stack | solution.py:99
  80.5 4.7 %convert_element_type.93 = bf16[32,40960]{1,0:T(8,128)(2,1)S(1)} reshape(bf16[1024,5,256]{2,1,0:T(8,128)(2,1)} %copy.19) | data formatting | bytes 5242880 | tf_op jit(solution)/shard_map/convert_element_type | solution.py:156
  85.2 10.0 %reduce-scatter.3.cloned.1.call-done = bf16[16,48,256]{2,1,0:T(8,128)(2,1)} async-done(((bf16[16,48,1024]{2,1,0:T(8,128)(2,1)}), bf16[16,48,256]{2,1,0:T(8,128)(2,1)}) %reduce-scatter.3.cloned.1.call-update) | async-done | bytes 393232 | tf_op jit(solution)/shard_map/reduce_scatter | solution.py:143
  95.2 1.5 fusion.37
  101.7 2.2 %copy.18 = bf16[512,5,256]{2,1,0:T(8,128)(2,1)} copy(bf16[512,5,256]{2,0,1:T(8,128)(2,1)S(1)} %fusion.24) | data formatting | bytes 2621440 | tf_op jit(solution)/shard_map/stack | solution.py:99
  103.8 3.5 %convert_element_type.92 = bf16[32,20480]{1,0:T(8,128)(2,1)} reshape(bf16[512,5,256]{2,1,0:T(8,128)(2,1)} %copy.18) | data formatting | bytes 2621440 | tf_op jit(solution)/shard_map/convert_element_type | solution.py:156
  107.4 3.4 %pad_maximum_fusion = bf16[32,61440]{1,0:T(8,128)(2,1)} fusion(bf16[32,40960]{1,0:T(8,128)(2,1)S(1)} %convert_element_type.93, bf16[32,20480]{1,0:T(8,128)(2,1)} %convert_element_type.92), kind=kLoop, calls=%fused_computation.5 | loop fusion | flops 7864320 | bytes 7864320 | tf_op jit(solution)/shard_map/concatenate | solution.py:45
  110.8 5.4 %reshape.124 = bf16[15360,128]{1,0:T(8,128)(2,1)} reshape(bf16[32,61440]{1,0:T(8,128)(2,1)} %pad_maximum_fusion) | data formatting | bytes 7864320 | tf_op jit(solution)/shard_map/reshape | solution.py:47
  116.2 11.3 %all-reduce.5 = (f32[]{:T(128)}, f32[]{:T(128)}) all-reduce(f32[]{:T(128)} %get-tuple-element.35, f32[]{:T(128)} %get-tuple-element.34), channel_id=1, replica_groups=mesh['dp_0'=4,'dp_1'=4,'dp_2'=2,'section'=4] {'dp_0'}, use_global_device_ids=true, to_apply=%region_6.7 | all-reduce | flops 2 | bytes 16 | tf_op jit(solution)/shard_map/psum | solution.py:32
  127.6 11.1 %all-reduce.4 = (f32[]{:T(128)}, f32[]{:T(128)}) all-reduce(f32[]{:T(128)} %get-tuple-element.16, f32[]{:T(128)} %get-tuple-element.17), channel_id=1, replica_groups=mesh['dp_0'=4,'dp_1'=4,'dp_2'=2,'section'=4] {'dp_1'}, use_global_device_ids=true, to_apply=%region_7.8 | all-reduce | flops 2 | bytes 16 | tf_op jit(solution)/shard_map/psum | solution.py:32
  138.7 3.1 %all-reduce.6 = (f32[]{:T(128)}, f32[]{:T(128)}) all-reduce(f32[]{:T(128)} %get-tuple-element.14, f32[]{:T(128)} %get-tuple-element.15), channel_id=1, replica_groups=mesh['dp_0'=4,'dp_1'=4,'dp_2'=2,'section'=4] {'dp_2'}, use_global_device_ids=true, to_apply=%region_8.9 | all-reduce | flops 2 | bytes 16 | tf_op jit(solution)/shard_map/psum | solution.py:32
  141.7 9.6 %all-reduce.3 = (f32[1]{0:T(128)}, f32[1]{0:T(128)}) all-reduce(f32[1]{0:T(128)} %bitcast.23, f32[1]{0:T(128)} %bitcast.11), channel_id=1, replica_groups=mesh['dp_0'=4,'dp_1'=4,'dp_2'=2,'section'=4] {'section'}, use_global_device_ids=true, to_apply=%region_9.10 | all-reduce | flops 2 | bytes 16 | tf_op jit(solution)/shard_map/psum | solution.py:32
  151.4 1.9 maximum_multiply_fusion
  153.3 44.7 %reduce-scatter.5.cloned.1.call-done = bf16[480,128]{1,0:T(8,128)(2,1)} async-done(((bf16[15360,128]{1,0:T(8,128)(2,1)}), bf16[480,128]{1,0:T(8,128)(2,1)}) %reduce-scatter.5.cloned.1.call-update) | async-done | bytes 122896 | tf_op jit(solution)/shard_map/reduce_scatter | solution.py:48
  198.0 0.8 slice_convert_fusion.1
  199.5 0.9 slice_convert_fusion
  (80 shorter events, 20.5 us)
Async XLA Ops:
  7.2 88.0 %reduce-scatter.3.cloned.1.call-start = ((), (), s32[]{:S(2)}) async-start(), calls=%async_computation.3 | async-start | bytes 1966080 | tf_op jit(solution)/shard_map/reduce_scatter | solution.py:143
  20.9 6.3 %copy-start.7 = (bf16[16,48,512]{2,1,0:T(8,128)(2,1)}, bf16[16,48,512]{2,1,0:T(8,128)(2,1)S(1)}, u32[]{:S(2)}) copy-start(bf16[16,48,512]{2,1,0:T(8,128)(2,1)S(1)} %slice.110) | copy-start | bytes 2359300
  24.4 1.5 copy-start.15
  24.4 2.8 %copy-start.13 = (bf16[16,48,512]{2,1,0:T(8,128)(2,1)S(1)}, bf16[16,48,512]{2,1,0:T(8,128)(2,1)}, u32[]{:S(2)}) copy-start(bf16[16,48,512]{2,1,0:T(8,128)(2,1)} %slice.114) | copy-start | bytes 2359300
  24.4 2.8 %copy-start.21 = (bf16[5,512,256]{2,1,0:T(8,128)(2,1)S(1)}, bf16[5,512,256]{2,1,0:T(8,128)(2,1)}, u32[]{:S(2)}) copy-start(bf16[5,512,256]{2,1,0:T(8,128)(2,1)} %param.6) | copy-start | bytes 3932164
  27.2 1.1 copy-start.9
  27.6 1.2 copy-start.11
  29.3 0.8 copy-start.6
  56.6 4.1 %copy-start.1 = (bf16[96,8,4,256]{3,1,2,0:T(8,128)(2,1)}, bf16[96,8,4,256]{3,1,2,0:T(8,128)(2,1)S(1)}, u32[]{:S(2)}) copy-start(bf16[96,8,4,256]{3,1,2,0:T(8,128)(2,1)S(1)} %copy.23) | copy-start | bytes 4718596
  56.8 1.6 copy-start.3
  56.8 2.7 %copy-start = (bf16[5,1024,256]{2,1,0:T(8,128)(2,1)S(1)}, bf16[5,1024,256]{2,1,0:T(8,128)(2,1)}, u32[]{:S(2)}) copy-start(bf16[5,1024,256]{2,1,0:T(8,128)(2,1)} %param.7) | copy-start | bytes 7864324
  63.6 0.8 copy-start.17
  63.8 1.2 copy-start.19
  68.8 3.2 %copy-start.4 = (bf16[4,16,6,8,256]{4,3,0,2,1:T(8,128)(2,1)S(1)}, bf16[4,16,6,8,256]{4,3,0,2,1:T(8,128)(2,1)}, u32[]{:S(2)}) copy-start(bf16[4,16,6,8,256]{4,3,0,2,1:T(8,128)(2,1)} %copy-done.3) | copy-start | bytes 4718596
  68.8 3.2 %copy-start.18 = (bf16[16,48,256]{2,1,0:T(8,128)(2,1)S(1)}, bf16[16,48,256]{2,1,0:T(8,128)(2,1)}, u32[]{:S(2)}) copy-start(bf16[16,48,256]{2,1,0:T(8,128)(2,1)} %copy-done.17) | copy-start | bytes 1179652
  68.9 129.1 %reduce-scatter.5.cloned.1.call-start = ((), (), s32[]{:S(2)}) async-start(), calls=%async_computation.4 | async-start | bytes 4055040 | tf_op jit(solution)/shard_map/reduce_scatter | solution.py:48
  72.0 1.4 copy-start.5
  73.5 1.4 copy-start.2
  73.5 1.5 copy-start.20
  95.2 1.5 copy-start.8
  96.7 1.1 copy-start.16
  97.9 1.1 copy-start.14
  99.0 1.1 copy-start.10
  100.1 1.1 copy-start.12
Sparse Core Ops, SparseCore 0:
  69.0 26.1 reduce-scatter.2
  116.3 81.5 reduce-scatter.4
where the time goes:
time: 209 us; the launch traced here: 208 us
  blocking collectives  60 us (29%)
  waiting for transfers between devices  54.7 us (26%)
  local copies, waits for them, and re-layouts  46.6 us (22%)
  matrix products  16.4 us (8%)
  other arithmetic  15.4 us (7%)
  between operations  14.5 us (7%)
    reduce_scatter x1, waiting for transfers between devices, sum_packed(): lax.psum_scatter(lines, axis, tiled=True).reshape(-1)  44.7 us
    psum x4, blocking collectives, one_axis_at_a_time(): x = lax.psum(x, axis)  35.2 us
    all_to_all x1, blocking collectives, copy_for_each(): lax.all_to_all(jnp.broadcast_to(x[None], (count, *x.shape)), axis, 0, 0,...  24.9 us
    slice x5, local copies, waits for them, and re-layouts, conv_strided(): window = padded[:, tap:tap + 3 * frames - 2:3].reshape(-1, values.shape[2])  14.5 us
    reduce_scatter x1, waiting for transfers between devices, shards(): lax.psum_scatter(upstream_terms.astype(jnp.bfloat16), 'section', scatter_...  9.96 us
    unnamed x47, local copies, waits for them, and re-layouts  8.98 us
    another operation x2, local copies, waits for them, and re-layouts, weight_term(): return jnp.stack(pieces, axis=1)  5.81 us
    reshape x1, local copies, waits for them, and re-layouts, sum_packed(): jnp.pad(lines, ((0, 0), (0, span * 128 - lines.shape[1]))).reshape(-1, 128)  5.43 us
  transfers between devices with their start and end apart: 2, of which 2 were waited for; matrix products, arithmetic and copies ran while one was open for 8% of the time, Pallas kernels for 0%

commit v1 on v0

--- a/solution.py
+++ b/solution.py
@@ -9,6 +9,11 @@
 DP_SECTION = ("dp_0", "dp_1", "dp_2", "section")
 smooth_width = 0.1
 leak_slope = 0.1
+
+
+def lay_the_floor(shard_in, dev_axis):
+    shaped = lax.all_gather(shard_in, dev_axis)
+    return jnp.sum(shaped, axis=0)
 
 
 def copy_for_each(x, axis):
@@ -29,7 +34,7 @@
 
 def one_axis_at_a_time(x, axes):
     for axis in axes:
-        x = lax.psum(x, axis)
+        x = lay_the_floor(x, dev_axis=axis)
     return x
 
 

time: 209 us -> 208 us (level)
  waiting for transfers between devices: 54.7 us -> 39.7 us
  local copies, waits for them, and re-layouts: 46.6 us -> 58 us
  other arithmetic: 15.4 us -> 19.1 us
  blocking collectives: 60 us -> 57.4 us
    psum x4 -> x0, blocking collectives: 35.2 us -> none  [one_axis_at_a_time(): x = lax.psum(x, axis)]
    unnamed x0 -> x4, blocking collectives: none -> 32.5 us
    reduce_scatter x1, waiting for transfers between devices: 44.7 us -> 28.3 us  [sum_packed(): lax.psum_scatter(lines, axis, tiled=True).reshape(-1)]
    unnamed x47 -> x59, local copies, waits for them, and re-layouts: 8.98 us -> 20.6 us
    reduce_sum x0 -> x8, other arithmetic: none -> 4.81 us  [lay_the_floor(): return jnp.sum(shaped, axis=0)]
  transfers between devices with their start and end apart: 2 -> 2, of which waited for: 2 -> 2; matrix products, arithmetic and copies ran while one was open for 8% -> 17% of each run, Pallas kernels for 0% -> 0%
where the time goes in v1:
time: 208 us; the launch traced here: 207 us
  local copies, waits for them, and re-layouts  58 us (28%)
  blocking collectives  57.4 us (28%)
  waiting for transfers between devices  39.7 us (19%)
  other arithmetic  19.1 us (9%)
  matrix products  18 us (9%)
  between operations  14.4 us (7%)
    unnamed x4, blocking collectives  32.5 us
    reduce_scatter x1, waiting for transfers between devices, sum_packed(): lax.psum_scatter(lines, axis, tiled=True).reshape(-1)  28.3 us
    all_to_all x1, blocking collectives, copy_for_each(): lax.all_to_all(jnp.broadcast_to(x[None], (count, *x.shape)), axis, 0, 0,...  24.9 us
    unnamed x59, local copies, waits for them, and re-layouts  20.6 us
    slice x5, local copies, waits for them, and re-layouts, conv_strided(): window = padded[:, tap:tap + 3 * frames - 2:3].reshape(-1, values.shape[2])  14.5 us
    reduce_scatter x1, waiting for transfers between devices, shards(): lax.psum_scatter(upstream_terms.astype(jnp.bfloat16), 'section', scatter_...  11.3 us
    dot_general x10, matrix products, weight_term(): lax.dot_general(window, flat_delta, (((0,), (0,)), ((), ())), preferred_e...  6.75 us
    another operation x2, local copies, waits for them, and re-layouts, weight_term(): return jnp.stack(pieces, axis=1)  5.81 us
  transfers between devices with their start and end apart: 2, of which 2 were waited for; matrix products, arithmetic and copies ran while one was open for 17% of the time, Pallas kernels for 0%

profile of v1, /device:TPU:0, one launch (start us, length us, event | category | flops | bytes accessed | tf_op | source)
XLA Modules:
  0.0 206.9 jit_solution(15537374317017595011)
XLA Ops:
  7.2 2.6 %fusion.3 = bf16[16,148,512]{2,1,0:T(8,128)(2,1)S(1)} fusion(bf16[8,144,512]{2,1,0:T(8,128)(2,1)} %param.5, bf16[8,144,512]{2,1,0:T(8,128)(2,1)} %param.4), kind=kLoop, calls=%fused_computation.7 | loop fusion | flops 10911744 | bytes 4784128 | tf_op jit(solution)/shard_map/concatenate | solution.py:133
  9.9 3.4 %slice.116 = bf16[16,48,512]{2,1,0:T(8,128)(2,1)} slice(bf16[16,148,512]{2,1,0:T(8,128)(2,1)S(1)} %fusion.3), slice={[0:16:1], [3:145:3], [0:512:1]} | slice | bytes 1572864 | tf_op jit(solution)/shard_map/slice | solution.py:65
  13.2 3.2 %slice.114 = bf16[16,48,512]{2,1,0:T(8,128)(2,1)} slice(bf16[16,148,512]{2,1,0:T(8,128)(2,1)S(1)} %fusion.3), slice={[0:16:1], [2:144:3], [0:512:1]} | slice | bytes 1572864 | tf_op jit(solution)/shard_map/slice | solution.py:65
  16.5 3.3 %slice.112 = bf16[16,48,512]{2,1,0:T(8,128)(2,1)} slice(bf16[16,148,512]{2,1,0:T(8,128)(2,1)S(1)} %fusion.3), slice={[0:16:1], [1:143:3], [0:512:1]} | slice | bytes 1572864 | tf_op jit(solution)/shard_map/slice | solution.py:65
  20.9 3.5 %slice.118 = bf16[16,48,512]{2,1,0:T(8,128)(2,1)} slice(bf16[16,148,512]{2,1,0:T(8,128)(2,1)S(1)} %fusion.3), slice={[0:16:1], [4:146:3], [0:512:1]} | slice | bytes 1572864 | tf_op jit(solution)/shard_map/slice | solution.py:65
  24.4 1.5 fusion.68
  29.4 24.9 %all_to_all.5 = bf16[4,16,48,256]{3,2,1,0:T(8,128)(2,1)S(1)} all-to-all(bf16[4,16,48,256]{3,2,1,0:T(8,128)(2,1)S(1)} %broadcast_in_dim.16), channel_id=1, replica_groups=mesh['dp_0'=4,'dp_1'=4,'dp_2'=2,'section'=4] {'section'}, dimensions={0} | all-to-all | bytes 3145728 | tf_op jit(solution)/shard_map/all_to_all | solution.py:21
  65.6 2.0 add_convert_fusion
  67.9 1.7 fusion.75
  69.7 2.2 %fusion.17 = bf16[1024,5,256]{2,0,1:T(8,128)(2,1)S(1)} fusion(bf16[16,48,256]{2,1,0:T(8,128)(2,1)S(1)} %get-tuple-element.29, bf16[16,48,1024]{2,1,0:T(8,128)(2,1)} %bitcast.237), kind=kOutput, calls=%fused_computation.41 | convolution fusion | flops 402915328 | bytes 2490368 | tf_op jit(solution)/shard_map/dot_general | solution.py:100
  74.4 3.6 %copy.19 = bf16[1024,5,256]{2,1,0:T(8,128)(2,1)} copy(bf16[1024,5,256]{2,0,1:T(8,128)(2,1)S(1)} %fusion.11) | data formatting | bytes 5242880 | tf_op jit(solution)/shard_map/stack | solution.py:104
  78.0 4.7 %convert_element_type.93 = bf16[32,40960]{1,0:T(8,128)(2,1)S(1)} reshape(bf16[1024,5,256]{2,1,0:T(8,128)(2,1)} %copy.19) | data formatting | bytes 5242880 | tf_op jit(solution)/shard_map/convert_element_type | solution.py:161
  82.7 11.3 %reduce-scatter.3.cloned.1.call-done = bf16[16,48,256]{2,1,0:T(8,128)(2,1)} async-done(((bf16[16,48,1024]{2,1,0:T(8,128)(2,1)}), bf16[16,48,256]{2,1,0:T(8,128)(2,1)}) %reduce-scatter.3.cloned.1.call-update) | async-done | bytes 393232 | tf_op jit(solution)/shard_map/reduce_scatter | solution.py:148
  94.0 1.5 fusion.37
  100.5 2.2 %copy.18 = bf16[512,5,256]{2,1,0:T(8,128)(2,1)} copy(bf16[512,5,256]{2,0,1:T(8,128)(2,1)S(1)} %fusion.24) | data formatting | bytes 2621440 | tf_op jit(solution)/shard_map/stack | solution.py:104
  102.7 3.5 %convert_element_type.92 = bf16[32,20480]{1,0:T(8,128)(2,1)} reshape(bf16[512,5,256]{2,1,0:T(8,128)(2,1)} %copy.18) | data formatting | bytes 2621440 | tf_op jit(solution)/shard_map/convert_element_type | solution.py:161
  106.2 3.4 %pad_maximum_fusion = bf16[32,61440]{1,0:T(8,128)(2,1)} fusion(bf16[32,40960]{1,0:T(8,128)(2,1)S(1)} %convert_element_type.93, bf16[32,20480]{1,0:T(8,128)(2,1)} %convert_element_type.92), kind=kLoop, calls=%fused_computation.5 | loop fusion | flops 7864320 | bytes 7864320 | tf_op jit(solution)/shard_map/concatenate | solution.py:50
  109.7 5.4 %reshape.124 = bf16[15360,128]{1,0:T(8,128)(2,1)} reshape(bf16[32,61440]{1,0:T(8,128)(2,1)} %pad_maximum_fusion) | data formatting | bytes 7864320 | tf_op jit(solution)/shard_map/reshape | solution.py:52
  116.3 1.4 dynamic-update-slice
  117.7 1.4 dynamic-update-slice.4
  119.7 10.6 %all-reduce.13 = (f32[4]{0:T(128)S(1)}, f32[4]{0:T(128)S(1)}) all-reduce(f32[4]{0:T(128)S(1)} %dynamic-update-slice.4, f32[4]{0:T(128)S(1)} %dynamic-update-slice), channel_id=1, replica_groups=mesh['dp_0'=4,'dp_1'=4,'dp_2'=2,'section'=4] {'dp_0'}, use_global_device_ids=true, to_apply=%add.7 | all-reduce | flops 8 | bytes 64
  131.5 1.4 dynamic-update-slice.1
  132.9 1.4 dynamic-update-slice.5
  134.9 10.5 %all-reduce.12 = (f32[4]{0:T(128)S(1)}, f32[4]{0:T(128)S(1)}) all-reduce(f32[4]{0:T(128)S(1)} %dynamic-update-slice.5, f32[4]{0:T(128)S(1)} %dynamic-update-slice.1), channel_id=1, replica_groups=mesh['dp_0'=4,'dp_1'=4,'dp_2'=2,'section'=4] {'dp_1'}, use_global_device_ids=true, to_apply=%add.8 | all-reduce | flops 8 | bytes 64
  146.6 1.4 dynamic-update-slice.2
  148.0 1.4 dynamic-update-slice.6
  150.0 2.4 %all-reduce.14 = (f32[2]{0:T(128)S(1)}, f32[2]{0:T(128)S(1)}) all-reduce(f32[2]{0:T(128)S(1)} %dynamic-update-slice.6, f32[2]{0:T(128)S(1)} %dynamic-update-slice.2), channel_id=1, replica_groups=mesh['dp_0'=4,'dp_1'=4,'dp_2'=2,'section'=4] {'dp_2'}, use_global_device_ids=true, to_apply=%add.9 | all-reduce | flops 4 | bytes 32
  153.7 1.4 dynamic-update-slice.3
  155.1 1.4 dynamic-update-slice.7
  156.5 9.0 %all-reduce.11 = (f32[4]{0:T(128)S(1)}, f32[4]{0:T(128)S(1)}) all-reduce(f32[4]{0:T(128)S(1)} %dynamic-update-slice.7, f32[4]{0:T(128)S(1)} %dynamic-update-slice.3), channel_id=1, replica_groups=mesh['dp_0'=4,'dp_1'=4,'dp_2'=2,'section'=4] {'section'}, use_global_device_ids=true, to_apply=%add.10 | all-reduce | flops 8 | bytes 64
  166.6 1.9 maximum_multiply_fusion
  168.5 28.3 %reduce-scatter.5.cloned.1.call-done = bf16[480,128]{1,0:T(8,128)(2,1)} async-done(((bf16[15360,128]{1,0:T(8,128)(2,1)}), bf16[480,128]{1,0:T(8,128)(2,1)}) %reduce-scatter.5.cloned.1.call-update) | async-done | bytes 122896 | tf_op jit(solution)/shard_map/reduce_scatter | solution.py:53
  (100 shorter events, 34.5 us)
Async XLA Ops:
  7.2 86.8 %reduce-scatter.3.cloned.1.call-start = ((), (), s32[]{:S(2)}) async-start(), calls=%async_computation.3 | async-start | bytes 1966080 | tf_op jit(solution)/shard_map/reduce_scatter | solution.py:148
  20.9 6.3 %copy-start.3 = (bf16[16,48,512]{2,1,0:T(8,128)(2,1)}, bf16[16,48,512]{2,1,0:T(8,128)(2,1)S(1)}, u32[]{:S(2)}) copy-start(bf16[16,48,512]{2,1,0:T(8,128)(2,1)S(1)} %slice.110) | copy-start | bytes 2359300
  24.4 1.5 copy-start.11
  24.4 2.8 %copy-start.9 = (bf16[16,48,512]{2,1,0:T(8,128)(2,1)S(1)}, bf16[16,48,512]{2,1,0:T(8,128)(2,1)}, u32[]{:S(2)}) copy-start(bf16[16,48,512]{2,1,0:T(8,128)(2,1)} %slice.114) | copy-start | bytes 2359300
  24.4 2.8 %copy-start.13 = (bf16[5,512,256]{2,1,0:T(8,128)(2,1)S(1)}, bf16[5,512,256]{2,1,0:T(8,128)(2,1)}, u32[]{:S(2)}) copy-start(bf16[5,512,256]{2,1,0:T(8,128)(2,1)} %param.6) | copy-start | bytes 3932164
  27.2 1.1 copy-start.5
  27.6 1.2 copy-start.7
  56.1 1.4 copy-start.1
  56.1 2.3 %copy-start = (bf16[5,1024,256]{2,1,0:T(8,128)(2,1)S(1)}, bf16[5,1024,256]{2,1,0:T(8,128)(2,1)}, u32[]{:S(2)}) copy-start(bf16[5,1024,256]{2,1,0:T(8,128)(2,1)} %param.7) | copy-start | bytes 7864324
  67.6 129.2 %reduce-scatter.5.cloned.1.call-start = ((), (), s32[]{:S(2)}) async-start(), calls=%async_computation.4 | async-start | bytes 4055040 | tf_op jit(solution)/shard_map/reduce_scatter | solution.py:53
  69.7 2.2 %copy-start.2 = (bf16[4,16,6,8,256]{4,3,0,2,1:T(8,128)(2,1)S(1)}, bf16[4,16,6,8,256]{4,3,0,2,1:T(8,128)(2,1)}, u32[]{:S(2)}) copy-start(bf16[4,16,6,8,256]{4,3,0,2,1:T(8,128)(2,1)} %copy-done.1) | copy-start | bytes 4718596
  94.0 1.5 copy-start.4
  95.5 1.1 copy-start.12
  96.7 1.1 copy-start.10
  97.8 1.1 copy-start.6
  99.0 1.1 copy-start.8
  115.1 0.7 copy-start.17
  115.1 4.0 %copy-start.16 = (u32[128]{0:T(128)S(1)}, u32[128]{0:T(128)}, u32[]{:S(2)}) copy-start(u32[128]{0:T(128)} %constant.40) | copy-start | bytes 1540
  115.1 19.3 %copy-start.15 = (u32[128]{0:T(128)S(1)}, u32[128]{0:T(128)}, u32[]{:S(2)}) copy-start(u32[128]{0:T(128)} %constant.45) | copy-start | bytes 1540
  115.1 34.3 %copy-start.14 = (u32[128]{0:T(128)S(1)}, u32[128]{0:T(128)}, u32[]{:S(2)}) copy-start(u32[128]{0:T(128)} %constant.50) | copy-start | bytes 1540
Sparse Core Ops, SparseCore 0:
  67.8 26.2 reduce-scatter.2
  115.2 81.5 reduce-scatter.4
